TPU v7x, 256 devices: a whole 4x4x8 slice. The times are simulated.
256 devices in a mesh: gz: 16 (over x, y_hi, core), ta: 16 (over z, y_lo).
Axes of the slice: x: 4, y: 4 (y_hi: 2, y_lo: 2; y = y_hi * 2 + y_lo), z: 8, core: 2. Of those that a mesh axis runs over, the one named last changes fastest.
Arguments:
- base_links: float32 [4, 2, 3, 3, 32, 32, 128], P(None, None, None, None, 'gz', 'ta'), may hold values from -6 to 6
- smeared_links: float32 [4, 2, 3, 3, 32, 32, 128], P(None, None, None, None, 'gz', 'ta'), may hold values from -6 to 6
- top_force: float32 [4, 2, 3, 3, 32, 32, 128], P(None, None, None, None, 'gz', 'ta'), may hold values from -6 to 6
Outputs:
- base_force: float32 [4, 2, 3, 3, 32, 32, 128], P(None, None, None, None, 'gz', 'ta')
All inputs are finite; a program needn't handle non-finite values.
Results may differ from a plain program's by a relative error of at most 0.0001.
Values sent between devices are 32-bit elements; how exact they have to be, the bound alone decides.
A program may use at most 64 MiB of HBM per device.

v0:
```python
import jax
import jax.numpy as jnp
from jax import lax
from jax.experimental import pallas as pl
from jax.experimental.pallas import tpu as pltpu
from jax.sharding import PartitionSpec as P

MESH = pl.DeviceIdType.MESH
LY = 8
WEIGHT = 0.1
LANES = 128
LINK = 18
SKEW = 9


def masks():
    row = lax.broadcasted_iota(jnp.int32, (1, 8, LANES), 1)
    col = lax.broadcasted_iota(jnp.int32, (1, 8, LANES), 2) % LY
    return {
        "low": row < 4,
        "even": row % 2 == 0,
        "near": row % 4 < 2,
        "row": row,
        "first": col == 0,
        "last": col == LY - 1,
    }


def pick(mask, yes, no):
    return jnp.where(jnp.broadcast_to(mask, yes.shape), yes, no)


def rows(v, shift):
    return pltpu.roll(v, shift % 8, 1)


def fwd_x(v):
    return pltpu.roll(v, LANES - LY, 2)


def back_x(v):
    return pltpu.roll(v, LY, 2)


def fwd_y(m, v):
    return pick(m["last"], pltpu.roll(v, LY - 1, 2), pltpu.roll(v, LANES - 1, 2))


def back_y(m, v):
    return pick(m["first"], pltpu.roll(v, LANES - LY + 1, 2), pltpu.roll(v, 1, 2))


def fwd_xy(m, v):
    return pick(m["low"], fwd_x(v), fwd_y(m, v))


def back_xy(m, v):
    return pick(m["low"], back_x(v), back_y(m, v))


def split(v):
    return v[:9].reshape(3, 3, 8, LANES), v[9:].reshape(3, 3, 8, LANES)


def join(m):
    return jnp.concatenate([m[0].reshape(9, 8, LANES), m[1].reshape(9, 8, LANES)], axis=0)


def outer_sum(lefts, rights):
    total = None
    for left, right in zip(lefts, rights):
        term = left[:, None] * right[None, :]
        total = term if total is None else total + term
    return total


def columns(a):
    return [a[:, k] for k in range(3)]


def lines(a):
    return [a[k] for k in range(3)]


def product(left, right, sl, sr):
    (ar, ai), (br, bi) = left, right
    rr, ii = outer_sum(ar, br), outer_sum(ai, bi)
    ri, ir = outer_sum(ar, bi), outer_sum(ai, br)
    re = rr - ii if sl * sr > 0 else rr + ii
    if sl > 0 and sr > 0:
        im = ri + ir
    elif sl < 0 and sr > 0:
        im = ri - ir
    else:
        im = ir - ri
    return re, im


def mul(a, b):
    return product((columns(a[0]), columns(a[1])), (lines(b[0]), lines(b[1])), 1, 1)


def mul_dn(a, b):
    return product((lines(a[0]), lines(a[1])), (lines(b[0]), lines(b[1])), -1, 1)


def mul_nd(a, b):
    return product((columns(a[0]), columns(a[1])), (columns(b[0]), columns(b[1])), 1, -1)


def add(a, b):
    return a[0] + b[0], a[1] + b[1]


def sub(a, b):
    return a[0] - b[0], a[1] - b[1]


def flip(v):
    return jnp.stack([v[:, 0], v[:, 1], v[:, 2]], axis=0)


def dagger(a):
    return flip(a[0]), -flip(a[1])


def scaled(c, a):
    cr, ci = c
    return cr * a[0] - ci * a[1], cr * a[1] + ci * a[0]


def skew_parts(a):
    re, im = a
    out = [im[0, 0], im[1, 1], im[2, 2]]
    for i, j in ((0, 1), (0, 2), (1, 2)):
        out += [0.5 * (re[i, j] - re[j, i]), 0.5 * (im[i, j] + im[j, i])]
    return out


def skew_matrix(v):
    d0, d1, d2, r01, i01, r02, i02, r12, i12 = [v[k] for k in range(9)]
    zero = jnp.zeros_like(d0)
    re = jnp.stack([jnp.stack([zero, r01, r02]), jnp.stack([-r01, zero, r12]), jnp.stack([-r02, -r12, zero])])
    im = jnp.stack([jnp.stack([d0, i01, i02]), jnp.stack([i01, d1, i12]), jnp.stack([i02, i12, d2])])
    return re, im


def pack_sends(m, low, high, comps, send):
    send[0, :comps] = pick(m["near"], rows(low, -2), high)
    send[1, :comps] = pick(m["near"], high, rows(low, 2))
    send[2, :comps] = pick(m["even"], rows(low, -1), high)
    send[3, :comps] = pick(m["even"], rows(high, 4), rows(low, 1))


def copies(src_low_high, send, recv, corner, ssem, rsem, where):
    plan = (
        (send.at[0], recv.at[0], where[0]),
        (send.at[1, :, pl.ds(2, 6)], recv.at[1, :, pl.ds(2, 6)], where[1]),
        (send.at[2], recv.at[2], where[2]),
        (send.at[3, :, pl.ds(1, 7)], recv.at[3, :, pl.ds(1, 7)], where[3]),
        (src_low_high.at[1, :, pl.ds(2, 1)], corner.at[:, pl.ds(1, 1)], where[4]),
        (src_low_high.at[1, :, pl.ds(5, 1)], corner.at[:, pl.ds(3, 1)], where[5]),
    )
    order = (1, 3, 0, 2, 4, 5)
    return [
        pltpu.make_async_remote_copy(
            src_ref=plan[k][0],
            dst_ref=plan[k][1],
            send_sem=ssem.at[k],
            recv_sem=rsem.at[k],
            device_id=plan[k][2],
            device_id_type=MESH,
        )
        for k in order
    ]


def gather_into(m, low, high, recv, corner, ga, gb, gc, gd):
    at_zm, at_zp, at_tm, at_tp = recv[0], recv[1], recv[2], recv[3]
    diag = corner[...]
    row = m["row"]
    a0 = pick(m["low"], low, rows(high, 4))
    d0 = pick(m["low"], rows(low, 4), high)
    ga[0], gd[0] = a0, d0
    gb[0] = pick(m["low"], fwd_x(d0), pick(m["near"], rows(d0, -2), rows(at_zp, 2)))
    gc[0] = pick(m["low"], fwd_y(m, a0), pick(m["even"], rows(a0, -1), rows(at_tp, 1)))
    up_z = pick(m["near"], rows(low, -2), at_zp)
    up_t = pick(m["even"], rows(low, -1), at_tp)
    ga[1], gd[1] = low, high
    gb[1] = fwd_xy(m, high)
    gc[1] = pick(m["low"], up_z, up_t)
    d2 = rows(high, 4)
    ga[2], gd[2] = low, d2
    gb[2] = fwd_xy(m, d2)
    gc[2] = pick(m["low"], up_t, up_z)
    dz = pick(row < 2, rows(at_zm, -2), pick(row < 4, at_zm, pick(row < 6, rows(at_zm, 2), rows(at_zm, 4))))
    ga[3], gd[3] = at_zm, dz
    gb[3] = pick(row < 6, fwd_xy(m, dz), pick(m["even"], rows(at_zm, 3), rows(diag, -2 + 8)))
    dt = pick(m["low"], pick(m["even"], rows(at_tm, 3), rows(at_tm, 4)), pick(m["even"], rows(at_tm, -1), at_tm))
    ga[4], gd[4] = at_tm, dt
    gb[4] = pick(m["even"], fwd_xy(m, dt), pick(row < 2, rows(at_tm, 2), diag))


def scatter_sum(m, pa, pb, pc, pd, rim):
    a0, b0, c0, d0 = pa[0], pb[0], pc[0], pd[0]
    a1, b1, c1, d1 = pa[1], pb[1], pc[1], pd[1]
    a2, b2, c2, d2 = pa[2], pb[2], pc[2], pd[2]
    rz, rt = rim[0], rim[1]
    from_z = pick(m["near"], rz, rows(pick(m["low"], c1, c2), 2))
    from_t = pick(m["even"], rt, rows(pick(m["low"], c2, c1), 1))
    low = (a1 + a2) + (from_z + from_t)
    low = low + pick(m["low"], a0 + back_y(m, c0), rows(d0 + back_x(b0), 4))
    high = (d1 + back_xy(m, b1)) + rows(d2 + back_xy(m, b2), 4)
    z_part = a0 + pick(m["even"], rows(rt, 3), rows(c0, 1))
    t_part = d0 + pick(m["near"], rows(rz, -2), rows(b0, 2))
    high = high + pick(m["low"], rows(z_part, 4), t_part)
    return low, high


def staples(ga, gb, gc, gd, keep_t, keep_z, pa, pb, pc, pd, rim):
    def block(k, carry):
        a, b, c, d = split(ga[k]), split(gb[k]), split(gc[k]), split(gd[k])
        t = mul_dn(a, d)
        keep_t[k] = join(t)
        pb[k] = join(mul(t, c))
        pc[k] = join(mul_dn(t, b))
        z = mul_nd(c, b)
        keep_z[k] = join(z)
        pa[k] = join(mul(d, z))
        pd[k] = join(mul_nd(a, z))
        return carry

    lax.fori_loop(0, 3, block, 0)

    def edge(k, carry):
        a, b, d = split(ga[k + 3]), split(gb[k + 3]), split(gd[k + 3])
        t = mul_dn(a, d)
        keep_t[k + 3] = join(t)
        rim[k] = join(mul_dn(t, b))
        return carry

    lax.fori_loop(0, 2, edge, 0)


def staple_forces(ga, gb, gc, gd, keep_t, keep_z, sa, sd, wa, wb, wc, wd, pa, pb, pc, pd, rim):
    def block(k, carry):
        a, b, c, d = split(ga[k]), split(gb[k]), split(gc[k]), split(gd[k])
        va, vd = wa[k], wd[k]
        oa, ob, oc, od = skew_matrix(va), skew_matrix(wb[k]), skew_matrix(wc[k]), skew_matrix(vd)
        t, z = split(keep_t[k]), split(keep_z[k])
        n = mul_dn(a, mul(skew_matrix(va - vd), d))
        pb[k] = join(mul(sub(mul(t, oc), n), c))
        pc[k] = join(mul(sub(mul_dn(t, ob), dagger(n)), b))
        q = sub(mul(oc, z), mul(z, ob))
        pa[k] = join(add(mul(d, q), mul(od, split(sa[k]))))
        pd[k] = join(add(mul_nd(a, q), mul(oa, split(sd[k]))))
        return carry

    lax.fori_loop(0, 3, block, 0)

    def edge(k, carry):
        a, b, d = split(ga[k + 3]), split(gb[k + 3]), split(gd[k + 3])
        n = mul_dn(a, mul(skew_matrix(wa[k + 3] - wd[k + 3]), d))
        t = split(keep_t[k + 3])
        rim[k] = join(mul(sub(mul_dn(t, skew_matrix(wb[k + 3])), dagger(n)), b))
        return carry

    lax.fori_loop(0, 2, edge, 0)


def weights(h):
    hh = h * h
    r2 = 1.0 - hh * 0.5
    r4 = r2 + hh * hh * (1.0 / 24.0)
    r6 = r4 - hh * hh * hh * (1.0 / 720.0)
    i3 = h - h * hh * (1.0 / 6.0)
    i5 = i3 + h * hh * hh * (1.0 / 120.0)
    return (r6, i5), (r4, i5), (r4, i3), (r2, i3), (r2, h)


def exponent_parts(links, staple_sum, keep_b, keep_bb, keep_e, keep_s):
    def block(k, carry):
        u, c = split(links[k]), split(staple_sum[k])
        omega = mul_nd(c, u)
        parts = [WEIGHT * v for v in skew_parts(omega)]
        h = (parts[0] + parts[1] + parts[2]) * (1.0 / 3.0)
        parts = jnp.stack([v - h for v in parts[:3]] + parts[3:])
        b = skew_matrix(parts)
        bb = mul(b, b)
        p = 0.5 * (bb[0][0, 0] + bb[0][1, 1] + bb[0][2, 2])
        s = jnp.sum((b[1] * bb[0] - b[0] * bb[1]).reshape(9, 8, LANES), axis=0) * (1.0 / 3.0)
        w0, w1, w2, w3, w4 = weights(h)
        pp, ps = p * p, p * s
        f0 = (
            w0[0] - s * w3[1] * (1.0 / 6.0) - ps * h * (1.0 / 120.0) - s * s * (1.0 / 720.0),
            w0[1] + s * w3[0] * (1.0 / 6.0) + ps * (1.0 / 120.0),
        )
        f1 = (
            w1[0] + p * w3[0] * (1.0 / 6.0) - s * w4[1] * (1.0 / 24.0) + pp * (1.0 / 120.0),
            w1[1] + p * w3[1] * (1.0 / 6.0) + s * w4[0] * (1.0 / 24.0) + pp * h * (1.0 / 120.0) + ps * (1.0 / 360.0),
        )
        f2 = (
            w2[0] * 0.5 + p * w4[0] * (1.0 / 24.0) - s * h * (1.0 / 120.0) + pp * (1.0 / 720.0),
            w2[1] * 0.5 + p * w4[1] * (1.0 / 24.0) + s * (1.0 / 120.0),
        )
        e = add(scaled(f1, b), scaled(f2, bb))
        unit = [[jnp.ones_like(p) if i == j else jnp.zeros_like(p) for j in range(3)] for i in range(3)]
        unit = jnp.stack([jnp.stack(r) for r in unit])
        e = e[0] + f0[0] * unit, e[1] + f0[1] * unit
        keep_b[k] = parts
        keep_bb[k] = join(bb)
        keep_e[k] = join(e)
        keep_s[k] = jnp.stack([p, s, h, f1[0], f1[1], f2[0], f2[1]])
        return carry

    lax.fori_loop(0, 2, block, 0)


def exponent_forces(links, staple_sum, force, keep_b, keep_bb, keep_e, keep_s, omega, direct):
    def block(k, carry):
        u, c, f = split(links[k]), split(staple_sum[k]), split(force[k])
        b, bb = skew_matrix(keep_b[k]), split(keep_bb[k])
        kept = keep_s[k]
        p, s, h = kept[0], kept[1], kept[2]
        f1, f2 = (kept[3], -kept[4]), (kept[5], -kept[6])
        d = mul_nd(f, u)

        def overlap(x):
            re = jnp.sum((d[0] * x[0] + d[1] * x[1]).reshape(9, 8, LANES), axis=0)
            im = jnp.sum((d[0] * x[1] - d[1] * x[0]).reshape(9, 8, LANES), axis=0)
            return re, im

        t0 = d[0][0, 0] + d[0][1, 1] + d[0][2, 2], -(d[1][0, 0] + d[1][1, 1] + d[1][2, 2])
        t1, t2 = overlap(b), overlap(bb)
        w0, w1, w2, w3, w4 = weights(h)
        pp, ps = p * p, p * s

        def slope(*changes):
            total = None
            for t, (re, im) in zip((t0, t1, t2), changes):
                term = t[0] * re - t[1] * im
                total = term if total is None else total + term
            return total

        gp = slope(
            (-s * h * (1.0 / 120.0), s * (1.0 / 120.0)),
            (w3[0] * (1.0 / 6.0) + p * (1.0 / 60.0), w3[1] * (1.0 / 6.0) + p * h * (1.0 / 60.0) + s * (1.0 / 360.0)),
            (w4[0] * (1.0 / 24.0) + p * (1.0 / 360.0), w4[1] * (1.0 / 24.0)),
        )
        gs = slope(
            (
                -w3[1] * (1.0 / 6.0) - p * h * (1.0 / 120.0) - s * (1.0 / 360.0),
                w3[0] * (1.0 / 6.0) + p * (1.0 / 120.0),
            ),
            (-w4[1] * (1.0 / 24.0), w4[0] * (1.0 / 24.0) + p * (1.0 / 360.0)),
            (-h * (1.0 / 120.0), jnp.full_like(h, 1.0 / 120.0)),
        )
        x0 = w1[0] - s * w4[1] * (1.0 / 6.0), w1[1] + s * w4[0] * (1.0 / 6.0) + ps * (1.0 / 120.0)
        x1 = (
            w2[0] + p * w4[0] * (1.0 / 6.0) - s * h * (1.0 / 24.0) + pp * (1.0 / 120.0),
            w2[1] + p * w4[1] * (1.0 / 6.0) + s * (1.0 / 24.0),
        )
        x2 = w3[0] * 0.5 + p * (1.0 / 24.0), w3[1] * 0.5 + p * h * (1.0 / 24.0) + s * (1.0 / 120.0)
        gh = slope(*[(-x[1], x[0]) for x in (x0, x1, x2)])
        d2 = scaled(f2, d)
        back = dagger(d2)
        half = 0.5 * (d2[0] + back[0]), 0.5 * (d2[1] + back[1])
        n = mul(b, half)
        d1 = scaled(f1, d)
        whole = (
            d1[0] - 2.0 * n[0] - gp * b[0] - gs * bb[1],
            d1[1] - 2.0 * n[1] - gp * b[1] + gs * bb[0],
        )
        parts = skew_parts(whole)
        shift = (gh - (parts[0] + parts[1] + parts[2])) * (1.0 / 3.0)
        parts = jnp.stack([WEIGHT * (v + shift) for v in parts[:3]] + [WEIGHT * v for v in parts[3:]])
        omega[k] = parts
        direct[k] = join(sub(mul_dn(split(keep_e[k]), f), mul(skew_matrix(parts), c)))
        return carry

    lax.fori_loop(0, 2, block, 0)


def kernel(counts, base_hbm, smeared_hbm, force_hbm, out_hbm, links, force, csum, direct, ga, gb, gc, gd, wa, wb, wc, wd,
           keep_t, keep_z, sa, sd, pa, pb, pc, pd, rim, keep_b, keep_bb, keep_e, keep_s, omega,
           send_u, recv_u, corner_u, send_w, recv_w, corner_w, in_sem, out_sem, send_sem, recv_sem):
    n_gz, n_ta = counts
    gz, ta = lax.axis_index("gz"), lax.axis_index("ta")
    zp, zm = lax.rem(gz + 1, n_gz), lax.rem(gz + n_gz - 1, n_gz)
    tp, tm = lax.rem(ta + 1, n_ta), lax.rem(ta + n_ta - 1, n_ta)
    where = ((zp, ta), (zm, ta), (gz, tp), (gz, tm), (zp, tm), (zm, tp))

    barrier = pltpu.get_barrier_semaphore()
    for device in where:
        pl.semaphore_signal(barrier, inc=1, device_id=device, device_id_type=MESH)

    def fetch(src, dst, slot):
        return [
            pltpu.make_async_copy(src.at[k], dst.at[k // 2, :, pl.ds(k % 2 * 4, 4)], in_sem.at[slot, k])
            for k in range(4)
        ]

    fetch_smeared = fetch(smeared_hbm, links.at[0], 0)
    fetch_base = fetch(base_hbm, links.at[1], 1)
    fetch_force = fetch(force_hbm, force, 2)
    for copy in fetch_smeared + fetch_base + fetch_force:
        copy.start()
    m = masks()

    def exchange(level, src, comps, send, recv, corner, slot):
        pack_sends(m, src[0], src[1], comps, send)
        moves = copies(src, send, recv, corner, send_sem.at[slot], recv_sem.at[slot], where)
        return moves

    for copy in fetch_smeared:
        copy.wait()
    moves_u0 = exchange(0, links.at[0], LINK, send_u.at[0], recv_u.at[0], corner_u.at[0], 0)
    pl.semaphore_wait(barrier, 6)
    for copy in moves_u0:
        copy.start()
    for copy in fetch_base:
        copy.wait()
    moves_u1 = exchange(1, links.at[1], LINK, send_u.at[1], recv_u.at[1], corner_u.at[1], 1)
    for copy in moves_u1:
        copy.start()
    for copy in fetch_force:
        copy.wait()

    def forward(level, moves):
        for copy in moves:
            copy.wait_recv()
        gather_into(m, links[level, 0], links[level, 1], recv_u.at[level], corner_u.at[level],
                    ga.at[level], gb.at[level], gc.at[level], gd.at[level])
        staples(ga.at[level], gb.at[level], gc.at[level], gd.at[level], keep_t.at[level], keep_z.at[level],
                sa.at[level], pb, pc, sd.at[level], rim)
        csum[level, 0], csum[level, 1] = scatter_sum(m, sa.at[level], pb, pc, sd.at[level], rim)
        exponent_parts(links.at[level], csum.at[level], keep_b.at[level], keep_bb.at[level], keep_e.at[level],
                       keep_s.at[level])

    def own_force(level):
        exponent_forces(links.at[level], csum.at[level], force, keep_b.at[level], keep_bb.at[level], keep_e.at[level],
                        keep_s.at[level], omega.at[level], direct)
        moves = exchange(level, omega.at[level], SKEW, send_w.at[level], recv_w.at[level], corner_w.at[level], 2 + level)
        for copy in moves:
            copy.start()
        return moves

    def finish(level, moves):
        for copy in moves:
            copy.wait_recv()
        gather_into(m, omega[level, 0], omega[level, 1], recv_w.at[level], corner_w.at[level], wa, wb, wc, wd)
        staple_forces(ga.at[level], gb.at[level], gc.at[level], gd.at[level], keep_t.at[level], keep_z.at[level],
                      sa.at[level], sd.at[level], wa, wb, wc, wd, pa, pb, pc, pd, rim)
        low, high = scatter_sum(m, pa, pb, pc, pd, rim)
        force[0] = low + direct[0]
        force[1] = high + direct[1]

    forward(0, moves_u0)
    moves_w0 = own_force(0)
    forward(1, moves_u1)
    finish(0, moves_w0)
    moves_w1 = own_force(1)
    finish(1, moves_w1)
    stores = [
        pltpu.make_async_copy(force.at[k // 2, :, pl.ds(k % 2 * 4, 4)], out_hbm.at[k], out_sem.at[k]) for k in range(4)
    ]
    for copy in stores:
        copy.start()
    for copy in moves_u0 + moves_u1 + moves_w0 + moves_w1:
        copy.wait_send()
    for copy in stores:
        copy.wait()


def solution(mesh):
    counts = (mesh.shape["gz"], mesh.shape["ta"])

    def vmem(*shape):
        return pltpu.VMEM(shape + (8, LANES), jnp.float32)

    def per_device(base_links, smeared_links, top_force):
        def flat(v):
            return v.reshape(4, LINK, 4, LANES)

        out = pl.pallas_call(
            lambda *refs: kernel(counts, *refs),
            out_shape=jax.ShapeDtypeStruct((4, LINK, 4, LANES), jnp.float32),
            in_specs=[pl.BlockSpec(memory_space=pl.ANY)] * 3,
            out_specs=pl.BlockSpec(memory_space=pl.ANY),
            scratch_shapes=[
                vmem(2, 2, LINK),
                vmem(2, LINK),
                vmem(2, 2, LINK),
                vmem(2, LINK),
                vmem(2, 5, LINK),
                vmem(2, 5, LINK),
                vmem(2, 3, LINK),
                vmem(2, 5, LINK),
                vmem(5, SKEW),
                vmem(5, SKEW),
                vmem(3, SKEW),
                vmem(5, SKEW),
                vmem(2, 5, LINK),
                vmem(2, 3, LINK),
                vmem(2, 3, LINK),
                vmem(2, 3, LINK),
                vmem(3, LINK),
                vmem(3, LINK),
                vmem(3, LINK),
                vmem(3, LINK),
                vmem(2, LINK),
                vmem(2, 2, SKEW),
                vmem(2, 2, LINK),
                vmem(2, 2, LINK),
                vmem(2, 2, 7),
                vmem(2, 2, SKEW),
                vmem(2, 4, LINK),
                vmem(2, 4, LINK),
                vmem(2, LINK),
                vmem(2, 4, SKEW),
                vmem(2, 4, SKEW),
                vmem(2, SKEW),
                pltpu.SemaphoreType.DMA((3, 4)),
                pltpu.SemaphoreType.DMA((4,)),
                pltpu.SemaphoreType.DMA((4, 6)),
                pltpu.SemaphoreType.DMA((4, 6)),
            ],
            compiler_params=pltpu.CompilerParams(
                collective_id=0, has_side_effects=True, vmem_limit_bytes=48 * 1024 * 1024
            ),
            name="stout_back",
        )(flat(base_links), flat(smeared_links), flat(top_force))
        return out.reshape(base_links.shape)

    spec = P(None, None, None, None, "gz", "ta", None)
    return jax.shard_map(per_device, mesh=mesh, in_specs=(spec, spec, spec), out_specs=spec, check_vma=False)
```

profile of v0, /device:TPU:1, one launch (start us, length us, event | category | flops | bytes accessed | tf_op | source)
XLA Modules:
  0.0 36.0 jit_solution(6841298734551672341)
XLA Ops:
  0.0 0.0 copy-start
  0.0 0.9 %copy-done = f32[4,2,3,3,2,2,128]{6,5,4,3,2,1,0:T(2,128)S(1)} copy-done((f32[4,2,3,3,2,2,128]{6,5,4,3,2,1,0:T(2,128)S(1)}, f32[4,2,3,3,2,2,128]{6,5,4,3,2,1,0:T(2,128)}, u32[]{:S(2)}) %copy-start) | copy-done | bytes 147480
  0.9 0.0 copy-start.1
  0.9 0.9 %copy-done.1 = f32[4,2,3,3,2,2,128]{6,5,4,3,2,1,0:T(2,128)S(1)} copy-done((f32[4,2,3,3,2,2,128]{6,5,4,3,2,1,0:T(2,128)S(1)}, f32[4,2,3,3,2,2,128]{6,5,4,3,2,1,0:T(2,128)}, u32[]{:S(2)}) %copy-start.1) | copy-done | bytes 147480
  1.8 0.0 copy-start.2
  1.8 0.9 %copy-done.2 = f32[4,2,3,3,2,2,128]{6,5,4,3,2,1,0:T(2,128)S(1)} copy-done((f32[4,2,3,3,2,2,128]{6,5,4,3,2,1,0:T(2,128)S(1)}, f32[4,2,3,3,2,2,128]{6,5,4,3,2,1,0:T(2,128)}, u32[]{:S(2)}) %copy-start.2) | copy-done | bytes 147480
  2.7 32.6 %stout_back.1 = f32[4,18,4,128]{3,2,1,0:T(4,128)S(1)} custom-call(f32[4,18,4,128]{3,2,1,0:T(4,128)S(1)} %bitcast.5, f32[4,18,4,128]{3,2,1,0:T(4,128)S(1)} %bitcast.6, f32[4,18,4,128]{3,2,1,0:T(4,128)S(1)} %bitcast.7), custom_call_target="tpu_custom_call" | custom-call | tf_op jit(solution)/shard_map/stout_back/pallas_call | solution.py:485
  35.4 0.7 %copy.5 = f32[4,2,3,3,2,2,128]{6,5,4,3,2,1,0:T(2,128)} copy(f32[4,2,3,3,2,2,128]{6,5,4,3,2,1,0:T(2,128)S(1)} %bitcast.4) | data formatting | bytes 294912
Async XLA Ops:
  0.0 0.9 %copy-start = (f32[4,2,3,3,2,2,128]{6,5,4,3,2,1,0:T(2,128)S(1)}, f32[4,2,3,3,2,2,128]{6,5,4,3,2,1,0:T(2,128)}, u32[]{:S(2)}) copy-start(f32[4,2,3,3,2,2,128]{6,5,4,3,2,1,0:T(2,128)} %param.3) | copy-start | bytes 442372
  0.9 0.9 %copy-start.1 = (f32[4,2,3,3,2,2,128]{6,5,4,3,2,1,0:T(2,128)S(1)}, f32[4,2,3,3,2,2,128]{6,5,4,3,2,1,0:T(2,128)}, u32[]{:S(2)}) copy-start(f32[4,2,3,3,2,2,128]{6,5,4,3,2,1,0:T(2,128)} %param.4) | copy-start | bytes 442372
  1.8 0.9 %copy-start.2 = (f32[4,2,3,3,2,2,128]{6,5,4,3,2,1,0:T(2,128)S(1)}, f32[4,2,3,3,2,2,128]{6,5,4,3,2,1,0:T(2,128)}, u32[]{:S(2)}) copy-start(f32[4,2,3,3,2,2,128]{6,5,4,3,2,1,0:T(2,128)} %param.5) | copy-start | bytes 442372
where the time goes:
time: 36.6 us; the launch traced here: 36 us
  Pallas kernels  32.6 us (89%)
  local copies, waits for them, and re-layouts  3.39 us (9%)
    pallas_call x1, Pallas kernels, per_device(): pl.pallas_call(lambda *refs: kernel(counts, *refs), out_shape=jax.ShapeDt...  32.6 us
    unnamed x7, local copies, waits for them, and re-layouts  3.39 us

commit v1 on v0

--- a/solution.py
+++ b/solution.py
@@ -152,50 +152,86 @@
     send[3, :comps] = pick(m["even"], rows(high, 4), rows(low, 1))
 
 
-def copies(src_low_high, send, recv, corner, ssem, rsem, where):
-    plan = (
-        (send.at[0], recv.at[0], where[0]),
-        (send.at[1, :, pl.ds(2, 6)], recv.at[1, :, pl.ds(2, 6)], where[1]),
-        (send.at[2], recv.at[2], where[2]),
-        (send.at[3, :, pl.ds(1, 7)], recv.at[3, :, pl.ds(1, 7)], where[3]),
-        (src_low_high.at[1, :, pl.ds(2, 1)], corner.at[:, pl.ds(1, 1)], where[4]),
-        (src_low_high.at[1, :, pl.ds(5, 1)], corner.at[:, pl.ds(3, 1)], where[5]),
+def remote(src, dst, sems, k, device):
+    return pltpu.make_async_remote_copy(
+        src_ref=src, dst_ref=dst, send_sem=sems[0].at[k], recv_sem=sems[1].at[k], device_id=device, device_id_type=MESH
     )
-    order = (1, 3, 0, 2, 4, 5)
-    return [
-        pltpu.make_async_remote_copy(
-            src_ref=plan[k][0],
-            dst_ref=plan[k][1],
-            send_sem=ssem.at[k],
-            recv_sem=rsem.at[k],
-            device_id=plan[k][2],
-            device_id_type=MESH,
-        )
-        for k in order
+
+
+def link_copies(src, recv, corner, sems, where):
+    ahead, behind = [], []
+    k = 0
+
+    def put(out, direction, row, count, slot, to):
+        nonlocal k
+        dst = corner if slot > 3 else recv.at[slot]
+        out.append(
+            remote(src.at[direction, :, pl.ds(row, count)], dst.at[:, pl.ds(to, count)], sems, k, where[slot])
+        )
+        k += 1
+
+    put(behind, 2, 2, 1, 4, 1)
+    put(behind, 3, 1, 1, 5, 3)
+    for direction, to in ((0, 2), (1, 6), (3, 4)):
+        put(ahead, direction, 0, 2, 1, to)
+    for direction, to in ((0, 1), (1, 5), (2, 4)):
+        put(ahead, direction, 0, 1, 3, to)
+        put(ahead, direction, 2, 1, 3, to + 2)
+    for direction, to in ((0, 0), (2, 2), (1, 4), (3, 6)):
+        put(behind, direction, 2, 2, 0, to)
+    for direction, to in ((0, 0), (2, 1), (1, 4), (3, 5)):
+        put(behind, direction, 1, 1, 2, to)
+        put(behind, direction, 3, 1, 2, to + 2)
+    return ahead, behind
+
+
+def term_copies(src, send, recv, corner, sems, where):
+    behind = [
+        remote(src.at[1, :, pl.ds(2, 1)], corner.at[:, pl.ds(1, 1)], sems, 4, where[4]),
+        remote(src.at[1, :, pl.ds(5, 1)], corner.at[:, pl.ds(3, 1)], sems, 5, where[5]),
+        remote(send.at[0], recv.at[0], sems, 0, where[0]),
+        remote(send.at[2], recv.at[2], sems, 2, where[2]),
     ]
-
-
-def gather_into(m, low, high, recv, corner, ga, gb, gc, gd):
-    at_zm, at_zp, at_tm, at_tp = recv[0], recv[1], recv[2], recv[3]
-    diag = corner[...]
-    row = m["row"]
-    a0 = pick(m["low"], low, rows(high, 4))
-    d0 = pick(m["low"], rows(low, 4), high)
-    ga[0], gd[0] = a0, d0
+    ahead = [
+        remote(send.at[1, :, pl.ds(2, 6)], recv.at[1, :, pl.ds(2, 6)], sems, 1, where[1]),
+        remote(send.at[3, :, pl.ds(1, 7)], recv.at[3, :, pl.ds(1, 7)], sems, 3, where[3]),
+    ]
+    return ahead, behind
+
+
+def start(moves):
+    ahead, behind = moves
+    for copy in behind[:2] + ahead + behind[2:]:
+        copy.start()
+
+
+def gather_own(m, low, high, ga, gb, gd):
+    ga[0], gd[0] = pick(m["low"], low, rows(high, 4)), pick(m["low"], rows(low, 4), high)
+    ga[1], gd[1] = low, high
+    gb[1] = fwd_xy(m, high)
+    d2 = rows(high, 4)
+    ga[2], gd[2] = low, d2
+    gb[2] = fwd_xy(m, d2)
+
+
+def gather_ahead(m, recv, ga, gb, gc, gd):
+    at_zp, at_tp = recv[1], recv[3]
+    a0, d0, low = ga[0], gd[0], ga[1]
     gb[0] = pick(m["low"], fwd_x(d0), pick(m["near"], rows(d0, -2), rows(at_zp, 2)))
     gc[0] = pick(m["low"], fwd_y(m, a0), pick(m["even"], rows(a0, -1), rows(at_tp, 1)))
     up_z = pick(m["near"], rows(low, -2), at_zp)
     up_t = pick(m["even"], rows(low, -1), at_tp)
-    ga[1], gd[1] = low, high
-    gb[1] = fwd_xy(m, high)
     gc[1] = pick(m["low"], up_z, up_t)
-    d2 = rows(high, 4)
-    ga[2], gd[2] = low, d2
-    gb[2] = fwd_xy(m, d2)
     gc[2] = pick(m["low"], up_t, up_z)
+
+
+def gather_behind(m, recv, corner, ga, gb, gd):
+    at_zm, at_tm = recv[0], recv[2]
+    diag = corner[...]
+    row = m["row"]
     dz = pick(row < 2, rows(at_zm, -2), pick(row < 4, at_zm, pick(row < 6, rows(at_zm, 2), rows(at_zm, 4))))
     ga[3], gd[3] = at_zm, dz
-    gb[3] = pick(row < 6, fwd_xy(m, dz), pick(m["even"], rows(at_zm, 3), rows(diag, -2 + 8)))
+    gb[3] = pick(row < 6, fwd_xy(m, dz), pick(m["even"], rows(at_zm, 3), rows(diag, 6)))
     dt = pick(m["low"], pick(m["even"], rows(at_tm, 3), rows(at_tm, 4)), pick(m["even"], rows(at_tm, -1), at_tm))
     ga[4], gd[4] = at_tm, dt
     gb[4] = pick(m["even"], fwd_xy(m, dt), pick(row < 2, rows(at_tm, 2), diag))
@@ -217,55 +253,85 @@
     return low, high
 
 
-def staples(ga, gb, gc, gd, keep_t, keep_z, pa, pb, pc, pd, rim):
-    def block(k, carry):
-        a, b, c, d = split(ga[k]), split(gb[k]), split(gc[k]), split(gd[k])
-        t = mul_dn(a, d)
+def each(first, last, body):
+    def step(k, carry):
+        body(k)
+        return carry
+
+    lax.fori_loop(first, last, step, 0)
+
+
+def staples_own(ga, gb, gd, keep_t, pc):
+    def corner_products(k):
+        keep_t[k] = join(mul_dn(split(ga[k]), split(gd[k])))
+
+    def ends(k):
+        pc[k] = join(mul_dn(split(keep_t[k]), split(gb[k])))
+
+    each(0, 3, corner_products)
+    each(1, 3, ends)
+
+
+def staples_ahead(ga, gb, gc, gd, keep_t, keep_z, pa, pb, pc, pd):
+    pc[0] = join(mul_dn(split(keep_t[0]), split(gb[0])))
+
+    def block(k):
+        c = split(gc[k])
+        pb[k] = join(mul(split(keep_t[k]), c))
+        z = mul_nd(c, split(gb[k]))
+        keep_z[k] = join(z)
+        pa[k] = join(mul(split(gd[k]), z))
+        pd[k] = join(mul_nd(split(ga[k]), z))
+
+    each(0, 3, block)
+
+
+def staples_behind(ga, gb, gd, keep_t, rim):
+    def block(k):
+        t = mul_dn(split(ga[k]), split(gd[k]))
         keep_t[k] = join(t)
-        pb[k] = join(mul(t, c))
-        pc[k] = join(mul_dn(t, b))
-        z = mul_nd(c, b)
-        keep_z[k] = join(z)
-        pa[k] = join(mul(d, z))
-        pd[k] = join(mul_nd(a, z))
-        return carry
-
-    lax.fori_loop(0, 3, block, 0)
-
-    def edge(k, carry):
-        a, b, d = split(ga[k + 3]), split(gb[k + 3]), split(gd[k + 3])
-        t = mul_dn(a, d)
-        keep_t[k + 3] = join(t)
-        rim[k] = join(mul_dn(t, b))
-        return carry
-
-    lax.fori_loop(0, 2, edge, 0)
-
-
-def staple_forces(ga, gb, gc, gd, keep_t, keep_z, sa, sd, wa, wb, wc, wd, pa, pb, pc, pd, rim):
-    def block(k, carry):
-        a, b, c, d = split(ga[k]), split(gb[k]), split(gc[k]), split(gd[k])
+        rim[k - 3] = join(mul_dn(t, split(gb[k])))
+
+    each(3, 5, block)
+
+
+def forces_own(ga, gb, gd, keep_t, keep_z, sa, sd, wa, wb, wd, keep_n, zb, pa, pc, pd):
+    def block(k):
         va, vd = wa[k], wd[k]
-        oa, ob, oc, od = skew_matrix(va), skew_matrix(wb[k]), skew_matrix(wc[k]), skew_matrix(vd)
-        t, z = split(keep_t[k]), split(keep_z[k])
-        n = mul_dn(a, mul(skew_matrix(va - vd), d))
-        pb[k] = join(mul(sub(mul(t, oc), n), c))
-        pc[k] = join(mul(sub(mul_dn(t, ob), dagger(n)), b))
-        q = sub(mul(oc, z), mul(z, ob))
-        pa[k] = join(add(mul(d, q), mul(od, split(sa[k]))))
-        pd[k] = join(add(mul_nd(a, q), mul(oa, split(sd[k]))))
-        return carry
-
-    lax.fori_loop(0, 3, block, 0)
-
-    def edge(k, carry):
-        a, b, d = split(ga[k + 3]), split(gb[k + 3]), split(gd[k + 3])
-        n = mul_dn(a, mul(skew_matrix(wa[k + 3] - wd[k + 3]), d))
-        t = split(keep_t[k + 3])
-        rim[k] = join(mul(sub(mul_dn(t, skew_matrix(wb[k + 3])), dagger(n)), b))
-        return carry
-
-    lax.fori_loop(0, 2, edge, 0)
+        keep_n[k] = join(mul_dn(split(ga[k]), mul(skew_matrix(va - vd), split(gd[k]))))
+        pa[k] = join(mul(skew_matrix(vd), split(sa[k])))
+        pd[k] = join(mul(skew_matrix(va), split(sd[k])))
+
+    each(0, 3, block)
+    each(1, 3, lambda k: force_end(gb, keep_t, keep_z, wb, keep_n, zb, pc, k))
+
+
+def force_end(gb, keep_t, keep_z, wb, keep_n, zb, pc, k):
+    ob = skew_matrix(wb[k])
+    pc[k] = join(mul(sub(mul_dn(split(keep_t[k]), ob), dagger(split(keep_n[k]))), split(gb[k])))
+    zb[k] = join(mul(split(keep_z[k]), ob))
+
+
+def forces_ahead(ga, gb, gc, gd, keep_t, keep_z, wb, wc, keep_n, zb, pa, pb, pc, pd):
+    force_end(gb, keep_t, keep_z, wb, keep_n, zb, pc, 0)
+
+    def block(k):
+        oc = skew_matrix(wc[k])
+        pb[k] = join(mul(sub(mul(split(keep_t[k]), oc), split(keep_n[k])), split(gc[k])))
+        q = sub(mul(oc, split(keep_z[k])), split(zb[k]))
+        pa[k] = join(add(mul(split(gd[k]), q), split(pa[k])))
+        pd[k] = join(add(mul_nd(split(ga[k]), q), split(pd[k])))
+
+    each(0, 3, block)
+
+
+def forces_behind(ga, gb, gd, keep_t, wa, wb, wd, rim):
+    def block(k):
+        n = mul_dn(split(ga[k]), mul(skew_matrix(wa[k] - wd[k]), split(gd[k])))
+        t = split(keep_t[k])
+        rim[k - 3] = join(mul(sub(mul_dn(t, skew_matrix(wb[k])), dagger(n)), split(gb[k])))
+
+    each(3, 5, block)
 
 
 def weights(h):
@@ -316,9 +382,9 @@
     lax.fori_loop(0, 2, block, 0)
 
 
-def exponent_forces(links, staple_sum, force, keep_b, keep_bb, keep_e, keep_s, omega, direct):
+def exponent_forces(links, force, keep_b, keep_bb, keep_s, omega):
     def block(k, carry):
-        u, c, f = split(links[k]), split(staple_sum[k]), split(force[k])
+        u, f = split(links[k]), split(force[k])
         b, bb = skew_matrix(keep_b[k]), split(keep_bb[k])
         kept = keep_s[k]
         p, s, h = kept[0], kept[1], kept[2]
@@ -375,15 +441,22 @@
         shift = (gh - (parts[0] + parts[1] + parts[2])) * (1.0 / 3.0)
         parts = jnp.stack([WEIGHT * (v + shift) for v in parts[:3]] + [WEIGHT * v for v in parts[3:]])
         omega[k] = parts
-        direct[k] = join(sub(mul_dn(split(keep_e[k]), f), mul(skew_matrix(parts), c)))
         return carry
 
     lax.fori_loop(0, 2, block, 0)
 
 
+def direct_forces(staple_sum, force, keep_e, omega, direct):
+    def block(k):
+        own = mul_dn(split(keep_e[k]), split(force[k]))
+        direct[k] = join(sub(own, mul(skew_matrix(omega[k]), split(staple_sum[k]))))
+
+    each(0, 2, block)
+
+
 def kernel(counts, base_hbm, smeared_hbm, force_hbm, out_hbm, links, force, csum, direct, ga, gb, gc, gd, wa, wb, wc, wd,
-           keep_t, keep_z, sa, sd, pa, pb, pc, pd, rim, keep_b, keep_bb, keep_e, keep_s, omega,
-           send_u, recv_u, corner_u, send_w, recv_w, corner_w, in_sem, out_sem, send_sem, recv_sem):
+           keep_t, keep_z, sa, sd, keep_n, zb, pa, pb, pc, pd, rim, keep_b, keep_bb, keep_e, keep_s, omega,
+           recv_u, corner_u, send_w, recv_w, corner_w, in_sem, out_sem, send_u_sem, recv_u_sem, send_w_sem, recv_w_sem):
     n_gz, n_ta = counts
     gz, ta = lax.axis_index("gz"), lax.axis_index("ta")
     zp, zm = lax.rem(gz + 1, n_gz), lax.rem(gz + n_gz - 1, n_gz)
@@ -400,74 +473,88 @@
             for k in range(4)
         ]
 
-    fetch_smeared = fetch(smeared_hbm, links.at[0], 0)
-    fetch_base = fetch(base_hbm, links.at[1], 1)
-    fetch_force = fetch(force_hbm, force, 2)
-    for copy in fetch_smeared + fetch_base + fetch_force:
+    fetches = fetch(smeared_hbm, links.at[0], 0) + fetch(base_hbm, links.at[1], 1) + fetch(force_hbm, force, 2)
+    for copy in fetches:
         copy.start()
     m = masks()
-
-    def exchange(level, src, comps, send, recv, corner, slot):
-        pack_sends(m, src[0], src[1], comps, send)
-        moves = copies(src, send, recv, corner, send_sem.at[slot], recv_sem.at[slot], where)
+    moves_u = [
+        link_copies(
+            src, recv_u.at[level], corner_u.at[level], (send_u_sem.at[level], recv_u_sem.at[level]), where
+        )
+        for level, src in ((0, smeared_hbm), (1, base_hbm))
+    ]
+    pl.semaphore_wait(barrier, 6)
+    for moves in moves_u:
+        start(moves)
+    for copy in fetches:
+        copy.wait()
+
+    def of(level, *refs):
+        return [r.at[level] for r in refs]
+
+    def landed(copies):
+        for copy in copies:
+            copy.wait_recv()
+
+    def before(level):
+        la, lb, ld, lt = of(level, ga, gb, gd, keep_t)
+        gather_own(m, links[level, 0], links[level, 1], la, lb, ld)
+        staples_own(la, lb, ld, lt, pc.at[level])
+
+    def forward(level):
+        la, lb, lc, ld, lt, lz = of(level, ga, gb, gc, gd, keep_t, keep_z)
+        ahead, behind = moves_u[level]
+        landed(ahead)
+        gather_ahead(m, recv_u.at[level], la, lb, lc, ld)
+        staples_ahead(la, lb, lc, ld, lt, lz, sa.at[level], pb, pc.at[level], sd.at[level])
+        landed(behind)
+        gather_behind(m, recv_u.at[level], corner_u.at[level], la, lb, ld)
+        staples_behind(la, lb, ld, lt, rim)
+        csum[level, 0], csum[level, 1] = scatter_sum(m, sa.at[level], pb, pc.at[level], sd.at[level], rim)
+        exponent_parts(links.at[level], csum.at[level], *of(level, keep_b, keep_bb, keep_e, keep_s))
+
+    def send_force(level):
+        exponent_forces(links.at[level], force, *of(level, keep_b, keep_bb, keep_s, omega))
+        pack_sends(m, omega[level, 0], omega[level, 1], SKEW, send_w.at[level])
+        moves = term_copies(
+            omega.at[level], send_w.at[level], recv_w.at[level], corner_w.at[level],
+            (send_w_sem.at[level], recv_w_sem.at[level]), where,
+        )
+        start(moves)
         return moves
 
-    for copy in fetch_smeared:
-        copy.wait()
-    moves_u0 = exchange(0, links.at[0], LINK, send_u.at[0], recv_u.at[0], corner_u.at[0], 0)
-    pl.semaphore_wait(barrier, 6)
-    for copy in moves_u0:
-        copy.start()
-    for copy in fetch_base:
-        copy.wait()
-    moves_u1 = exchange(1, links.at[1], LINK, send_u.at[1], recv_u.at[1], corner_u.at[1], 1)
-    for copy in moves_u1:
-        copy.start()
-    for copy in fetch_force:
-        copy.wait()
-
-    def forward(level, moves):
-        for copy in moves:
-            copy.wait_recv()
-        gather_into(m, links[level, 0], links[level, 1], recv_u.at[level], corner_u.at[level],
-                    ga.at[level], gb.at[level], gc.at[level], gd.at[level])
-        staples(ga.at[level], gb.at[level], gc.at[level], gd.at[level], keep_t.at[level], keep_z.at[level],
-                sa.at[level], pb, pc, sd.at[level], rim)
-        csum[level, 0], csum[level, 1] = scatter_sum(m, sa.at[level], pb, pc, sd.at[level], rim)
-        exponent_parts(links.at[level], csum.at[level], keep_b.at[level], keep_bb.at[level], keep_e.at[level],
-                       keep_s.at[level])
-
-    def own_force(level):
-        exponent_forces(links.at[level], csum.at[level], force, keep_b.at[level], keep_bb.at[level], keep_e.at[level],
-                        keep_s.at[level], omega.at[level], direct)
-        moves = exchange(level, omega.at[level], SKEW, send_w.at[level], recv_w.at[level], corner_w.at[level], 2 + level)
-        for copy in moves:
-            copy.start()
-        return moves
-
-    def finish(level, moves):
-        for copy in moves:
-            copy.wait_recv()
-        gather_into(m, omega[level, 0], omega[level, 1], recv_w.at[level], corner_w.at[level], wa, wb, wc, wd)
-        staple_forces(ga.at[level], gb.at[level], gc.at[level], gd.at[level], keep_t.at[level], keep_z.at[level],
-                      sa.at[level], sd.at[level], wa, wb, wc, wd, pa, pb, pc, pd, rim)
-        low, high = scatter_sum(m, pa, pb, pc, pd, rim)
+    def finish(level, moves, meanwhile):
+        la, lb, lc, ld, lt, lz = of(level, ga, gb, gc, gd, keep_t, keep_z)
+        direct_forces(csum.at[level], force, keep_e.at[level], omega.at[level], direct)
+        gather_own(m, omega[level, 0], omega[level, 1], wa, wb, wd)
+        forces_own(la, lb, ld, lt, lz, sa.at[level], sd.at[level], wa, wb, wd, keep_n, zb, pa, pc.at[level], pd)
+        meanwhile()
+        ahead, behind = moves
+        landed(ahead)
+        gather_ahead(m, recv_w.at[level], wa, wb, wc, wd)
+        forces_ahead(la, lb, lc, ld, lt, lz, wb, wc, keep_n, zb, pa, pb, pc.at[level], pd)
+        landed(behind)
+        gather_behind(m, recv_w.at[level], corner_w.at[level], wa, wb, wd)
+        forces_behind(la, lb, ld, lt, wa, wb, wd, rim)
+        low, high = scatter_sum(m, pa, pb, pc.at[level], pd, rim)
         force[0] = low + direct[0]
         force[1] = high + direct[1]
 
-    forward(0, moves_u0)
-    moves_w0 = own_force(0)
-    forward(1, moves_u1)
-    finish(0, moves_w0)
-    moves_w1 = own_force(1)
-    finish(1, moves_w1)
+    before(0)
+    before(1)
+    forward(0)
+    moves_w0 = send_force(0)
+    finish(0, moves_w0, lambda: forward(1))
+    moves_w1 = send_force(1)
+    finish(1, moves_w1, lambda: None)
     stores = [
         pltpu.make_async_copy(force.at[k // 2, :, pl.ds(k % 2 * 4, 4)], out_hbm.at[k], out_sem.at[k]) for k in range(4)
     ]
     for copy in stores:
         copy.start()
-    for copy in moves_u0 + moves_u1 + moves_w0 + moves_w1:
-        copy.wait_send()
+    for ahead, behind in (*moves_u, moves_w0, moves_w1):
+        for copy in ahead + behind:
+            copy.wait_send()
     for copy in stores:
         copy.wait()
 
@@ -508,6 +595,8 @@
                 vmem(3, LINK),
                 vmem(3, LINK),
                 vmem(3, LINK),
+                vmem(2, 3, LINK),
+                vmem(3, LINK),
                 vmem(2, LINK),
                 vmem(2, 2, SKEW),
                 vmem(2, 2, LINK),
@@ -515,18 +604,19 @@
                 vmem(2, 2, 7),
                 vmem(2, 2, SKEW),
                 vmem(2, 4, LINK),
-                vmem(2, 4, LINK),
                 vmem(2, LINK),
                 vmem(2, 4, SKEW),
                 vmem(2, 4, SKEW),
                 vmem(2, SKEW),
                 pltpu.SemaphoreType.DMA((3, 4)),
                 pltpu.SemaphoreType.DMA((4,)),
-                pltpu.SemaphoreType.DMA((4, 6)),
-                pltpu.SemaphoreType.DMA((4, 6)),
+                pltpu.SemaphoreType.DMA((2, 23)),
+                pltpu.SemaphoreType.DMA((2, 23)),
+                pltpu.SemaphoreType.DMA((2, 6)),
+                pltpu.SemaphoreType.DMA((2, 6)),
             ],
             compiler_params=pltpu.CompilerParams(
-                collective_id=0, has_side_effects=True, vmem_limit_bytes=48 * 1024 * 1024
+                collective_id=0, has_side_effects=True, vmem_limit_bytes=67_043_328
             ),
             name="stout_back",
         )(flat(base_links), flat(smeared_links), flat(top_force))

time: 36.6 us -> 32.8 us (0.90); the launches traced: 36 us -> 32.7 us
  local copies, waits for them, and re-layouts: 3.39 us -> 1.59 us
  Pallas kernels: 32.6 us -> 31.1 us
    unnamed x7 -> x1, local copies, waits for them, and re-layouts: 3.39 us -> 1.59 us
    pallas_call x1, Pallas kernels: 32.6 us -> 31.1 us  [per_device(): pl.pallas_call(lambda *refs: kernel(counts, *refs), out_shape=jax.ShapeDt...]
where the time goes in v1:
time: 32.8 us; the launch traced here: 32.7 us
  Pallas kernels  31.1 us (95%)
  local copies, waits for them, and re-layouts  1.59 us (5%)
    pallas_call x1, Pallas kernels, per_device(): pl.pallas_call(lambda *refs: kernel(counts, *refs), out_shape=jax.ShapeDt...  31.1 us
    unnamed x1, local copies, waits for them, and re-layouts  1.59 us

profile of v1, /device:TPU:1, one launch (start us, length us, event | category | flops | bytes accessed | tf_op | source)
XLA Modules:
  0.0 32.7 jit_solution(4232894759585337888)
XLA Ops:
  0.0 31.1 %stout_back.1 = f32[4,18,4,128]{3,2,1,0:T(4,128)} custom-call(f32[4,18,4,128]{3,2,1,0:T(4,128)} %bitcast.5, f32[4,18,4,128]{3,2,1,0:T(4,128)} %bitcast.6, f32[4,18,4,128]{3,2,1,0:T(4,128)} %bitcast.7), custom_call_target="tpu_custom_call" | custom-call | tf_op jit(solution)/shard_map/stout_back/pallas_call | solution.py:572
  31.1 1.6 %copy.5 = f32[4,2,3,3,2,2,128]{6,5,4,3,2,1,0:T(2,128)} copy(f32[4,2,3,3,2,2,128]{6,5,4,3,2,1,0:T(2,128)} %bitcast.4) | data formatting | bytes 294912

commit v2 on v1

--- a/solution.py
+++ b/solution.py
@@ -237,19 +237,25 @@
     gb[4] = pick(m["even"], fwd_xy(m, dt), pick(row < 2, rows(at_tm, 2), diag))
 
 
-def scatter_sum(m, pa, pb, pc, pd, rim):
+def scatter_own(m, pa, pb, pc, pd):
     a0, b0, c0, d0 = pa[0], pb[0], pc[0], pd[0]
-    a1, b1, c1, d1 = pa[1], pb[1], pc[1], pd[1]
-    a2, b2, c2, d2 = pa[2], pb[2], pc[2], pd[2]
+    c1, c2 = pc[1], pc[2]
+    zero = jnp.zeros_like(a0)
+    from_z = pick(m["near"], zero, rows(pick(m["low"], c1, c2), 2))
+    from_t = pick(m["even"], zero, rows(pick(m["low"], c2, c1), 1))
+    low = (pa[1] + pa[2]) + (from_z + from_t)
+    low = low + pick(m["low"], a0 + back_y(m, c0), rows(d0 + back_x(b0), 4))
+    high = (pd[1] + back_xy(m, pb[1])) + rows(pd[2] + back_xy(m, pb[2]), 4)
+    z_part = a0 + pick(m["even"], zero, rows(c0, 1))
+    t_part = d0 + pick(m["near"], zero, rows(b0, 2))
+    return low, high + pick(m["low"], rows(z_part, 4), t_part)
+
+
+def scatter_rim(m, rim):
     rz, rt = rim[0], rim[1]
-    from_z = pick(m["near"], rz, rows(pick(m["low"], c1, c2), 2))
-    from_t = pick(m["even"], rt, rows(pick(m["low"], c2, c1), 1))
-    low = (a1 + a2) + (from_z + from_t)
-    low = low + pick(m["low"], a0 + back_y(m, c0), rows(d0 + back_x(b0), 4))
-    high = (d1 + back_xy(m, b1)) + rows(d2 + back_xy(m, b2), 4)
-    z_part = a0 + pick(m["even"], rows(rt, 3), rows(c0, 1))
-    t_part = d0 + pick(m["near"], rows(rz, -2), rows(b0, 2))
-    high = high + pick(m["low"], rows(z_part, 4), t_part)
+    zero = jnp.zeros_like(rz)
+    low = pick(m["near"], rz, zero) + pick(m["even"], rt, zero)
+    high = pick(m["low"], pick(m["even"], rows(rt, -1), zero), pick(m["near"], rows(rz, -2), zero))
     return low, high
 
 
@@ -382,14 +388,20 @@
     lax.fori_loop(0, 2, block, 0)
 
 
-def exponent_forces(links, force, keep_b, keep_bb, keep_s, omega):
+def force_products(links, force, keep_d):
+    def block(k):
+        keep_d[k] = join(mul_nd(split(force[k]), split(links[k])))
+
+    each(0, 2, block)
+
+
+def exponent_forces(keep_d, keep_b, keep_bb, keep_s, omega):
     def block(k, carry):
-        u, f = split(links[k]), split(force[k])
         b, bb = skew_matrix(keep_b[k]), split(keep_bb[k])
         kept = keep_s[k]
         p, s, h = kept[0], kept[1], kept[2]
         f1, f2 = (kept[3], -kept[4]), (kept[5], -kept[6])
-        d = mul_nd(f, u)
+        d = split(keep_d[k])
 
         def overlap(x):
             re = jnp.sum((d[0] * x[0] + d[1] * x[1]).reshape(9, 8, LANES), axis=0)
@@ -454,9 +466,9 @@
     each(0, 2, block)
 
 
-def kernel(counts, base_hbm, smeared_hbm, force_hbm, out_hbm, links, force, csum, direct, ga, gb, gc, gd, wa, wb, wc, wd,
-           keep_t, keep_z, sa, sd, keep_n, zb, pa, pb, pc, pd, rim, keep_b, keep_bb, keep_e, keep_s, omega,
-           recv_u, corner_u, send_w, recv_w, corner_w, in_sem, out_sem, send_u_sem, recv_u_sem, send_w_sem, recv_w_sem):
+def kernel(counts, base_hbm, smeared_hbm, force_hbm, out_ref, links, force, csum, direct, ga, gb, gc, gd, wa, wb, wc, wd,
+           keep_t, keep_z, sa, sd, keep_n, zb, pa, pb, pc, pd, rim, keep_b, keep_bb, keep_e, keep_s, keep_d, omega,
+           recv_u, corner_u, send_w, recv_w, corner_w, in_sem, send_u_sem, recv_u_sem, send_w_sem, recv_w_sem):
     n_gz, n_ta = counts
     gz, ta = lax.axis_index("gz"), lax.axis_index("ta")
     zp, zm = lax.rem(gz + 1, n_gz), lax.rem(gz + n_gz - 1, n_gz)
@@ -484,13 +496,16 @@
         for level, src in ((0, smeared_hbm), (1, base_hbm))
     ]
     pl.semaphore_wait(barrier, 6)
-    for moves in moves_u:
-        start(moves)
+    start(moves_u[0])
     for copy in fetches:
         copy.wait()
 
     def of(level, *refs):
         return [r.at[level] for r in refs]
+
+    def sent(moves):
+        for copy in moves[0] + moves[1]:
+            copy.wait_send()
 
     def landed(copies):
         for copy in copies:
@@ -507,14 +522,17 @@
         landed(ahead)
         gather_ahead(m, recv_u.at[level], la, lb, lc, ld)
         staples_ahead(la, lb, lc, ld, lt, lz, sa.at[level], pb, pc.at[level], sd.at[level])
+        csum[level, 0], csum[level, 1] = scatter_own(m, sa.at[level], pb, pc.at[level], sd.at[level])
         landed(behind)
         gather_behind(m, recv_u.at[level], corner_u.at[level], la, lb, ld)
         staples_behind(la, lb, ld, lt, rim)
-        csum[level, 0], csum[level, 1] = scatter_sum(m, sa.at[level], pb, pc.at[level], sd.at[level], rim)
+        low, high = scatter_rim(m, rim)
+        csum[level, 0] += low
+        csum[level, 1] += high
         exponent_parts(links.at[level], csum.at[level], *of(level, keep_b, keep_bb, keep_e, keep_s))
 
     def send_force(level):
-        exponent_forces(links.at[level], force, *of(level, keep_b, keep_bb, keep_s, omega))
+        exponent_forces(keep_d, *of(level, keep_b, keep_bb, keep_s, omega))
         pack_sends(m, omega[level, 0], omega[level, 1], SKEW, send_w.at[level])
         moves = term_copies(
             omega.at[level], send_w.at[level], recv_w.at[level], corner_w.at[level],
@@ -533,30 +551,33 @@
         landed(ahead)
         gather_ahead(m, recv_w.at[level], wa, wb, wc, wd)
         forces_ahead(la, lb, lc, ld, lt, lz, wb, wc, keep_n, zb, pa, pb, pc.at[level], pd)
+        low, high = scatter_own(m, pa, pb, pc.at[level], pd)
+        direct[0] += low
+        direct[1] += high
         landed(behind)
         gather_behind(m, recv_w.at[level], corner_w.at[level], wa, wb, wd)
         forces_behind(la, lb, ld, lt, wa, wb, wd, rim)
-        low, high = scatter_sum(m, pa, pb, pc.at[level], pd, rim)
-        force[0] = low + direct[0]
-        force[1] = high + direct[1]
-
+        low, high = scatter_rim(m, rim)
+        low, high = low + direct[0], high + direct[1]
+        if level == 0:
+            force[0], force[1] = low, high
+        else:
+            out_ref[0], out_ref[1] = low[:, :4], low[:, 4:]
+            out_ref[2], out_ref[3] = high[:, :4], high[:, 4:]
+
+    force_products(links.at[0], force, keep_d)
     before(0)
     before(1)
+    sent(moves_u[0])
+    start(moves_u[1])
     forward(0)
     moves_w0 = send_force(0)
     finish(0, moves_w0, lambda: forward(1))
+    force_products(links.at[1], force, keep_d)
     moves_w1 = send_force(1)
     finish(1, moves_w1, lambda: None)
-    stores = [
-        pltpu.make_async_copy(force.at[k // 2, :, pl.ds(k % 2 * 4, 4)], out_hbm.at[k], out_sem.at[k]) for k in range(4)
-    ]
-    for copy in stores:
-        copy.start()
-    for ahead, behind in (*moves_u, moves_w0, moves_w1):
-        for copy in ahead + behind:
-            copy.wait_send()
-    for copy in stores:
-        copy.wait()
+    for moves in (moves_u[1], moves_w0, moves_w1):
+        sent(moves)
 
 
 def solution(mesh):
@@ -573,7 +594,7 @@
             lambda *refs: kernel(counts, *refs),
             out_shape=jax.ShapeDtypeStruct((4, LINK, 4, LANES), jnp.float32),
             in_specs=[pl.BlockSpec(memory_space=pl.ANY)] * 3,
-            out_specs=pl.BlockSpec(memory_space=pl.ANY),
+            out_specs=pl.BlockSpec(memory_space=pltpu.VMEM),
             scratch_shapes=[
                 vmem(2, 2, LINK),
                 vmem(2, LINK),
@@ -602,6 +623,7 @@
                 vmem(2, 2, LINK),
                 vmem(2, 2, LINK),
                 vmem(2, 2, 7),
+                vmem(2, LINK),
                 vmem(2, 2, SKEW),
                 vmem(2, 4, LINK),
                 vmem(2, LINK),
@@ -609,17 +631,16 @@
                 vmem(2, 4, SKEW),
                 vmem(2, SKEW),
                 pltpu.SemaphoreType.DMA((3, 4)),
-                pltpu.SemaphoreType.DMA((4,)),
                 pltpu.SemaphoreType.DMA((2, 23)),
                 pltpu.SemaphoreType.DMA((2, 23)),
                 pltpu.SemaphoreType.DMA((2, 6)),
                 pltpu.SemaphoreType.DMA((2, 6)),
             ],
             compiler_params=pltpu.CompilerParams(
-                collective_id=0, has_side_effects=True, vmem_limit_bytes=67_043_328
+                collective_id=0, has_side_effects=True, vmem_limit_bytes=48 * 1024 * 1024
             ),
             name="stout_back",
-        )(flat(base_links), flat(smeared_links), flat(top_force))
+        )(*[pltpu.with_memory_space_constraint(flat(v), pltpu.HBM) for v in (base_links, smeared_links, top_force)])
         return out.reshape(base_links.shape)
 
     spec = P(None, None, None, None, "gz", "ta", None)

time: 32.8 us -> 30.4 us (0.927)
  Pallas kernels: 31.1 us -> 29.6 us
  local copies, waits for them, and re-layouts: 1.59 us -> 0.66 us
    pallas_call x1, Pallas kernels: 31.1 us -> 29.6 us  [per_device(): pl.pallas_call(lambda *refs: kernel(counts, *refs), out_shape=jax.ShapeDt...]
    unnamed x1, local copies, waits for them, and re-layouts: 1.59 us -> 0.66 us
where the time goes in v2:
time: 30.4 us; the launch traced here: 30.3 us
  Pallas kernels  29.6 us (97%)
  local copies, waits for them, and re-layouts  0.66 us (2%)
    pallas_call x1, Pallas kernels, per_device(): pl.pallas_call(lambda *refs: kernel(counts, *refs), out_shape=jax.ShapeDt...  29.6 us
    unnamed x1, local copies, waits for them, and re-layouts  0.66 us

profile of v2, /device:TPU:1, one launch (start us, length us, event | category | flops | bytes accessed | tf_op | source)
XLA Modules:
  0.0 30.3 jit_solution(16535242259893525340)
XLA Ops:
  0.0 29.6 %stout_back.1 = f32[4,18,4,128]{3,2,1,0:T(4,128)S(1)} custom-call(f32[4,18,4,128]{3,2,1,0:T(4,128)} %bitcast.5, f32[4,18,4,128]{3,2,1,0:T(4,128)} %bitcast.6, f32[4,18,4,128]{3,2,1,0:T(4,128)} %bitcast.7), custom_call_target="tpu_custom_call" | custom-call | tf_op jit(solution)/shard_map/stout_back/pallas_call | solution.py:593
  29.6 0.7 %copy.5 = f32[4,2,3,3,2,2,128]{6,5,4,3,2,1,0:T(2,128)} copy(f32[4,2,3,3,2,2,128]{6,5,4,3,2,1,0:T(2,128)S(1)} %bitcast.4) | data formatting | bytes 294912

commit v3 on v2

--- a/solution.py
+++ b/solution.py
@@ -172,16 +172,16 @@
 
     put(behind, 2, 2, 1, 4, 1)
     put(behind, 3, 1, 1, 5, 3)
-    for direction, to in ((0, 2), (1, 6), (3, 4)):
-        put(ahead, direction, 0, 2, 1, to)
     for direction, to in ((0, 1), (1, 5), (2, 4)):
         put(ahead, direction, 0, 1, 3, to)
         put(ahead, direction, 2, 1, 3, to + 2)
-    for direction, to in ((0, 0), (2, 2), (1, 4), (3, 6)):
-        put(behind, direction, 2, 2, 0, to)
+    for direction, to in ((0, 2), (1, 6), (3, 4)):
+        put(ahead, direction, 0, 2, 1, to)
     for direction, to in ((0, 0), (2, 1), (1, 4), (3, 5)):
         put(behind, direction, 1, 1, 2, to)
         put(behind, direction, 3, 1, 2, to + 2)
+    for direction, to in ((0, 0), (2, 2), (1, 4), (3, 6)):
+        put(behind, direction, 2, 2, 0, to)
     return ahead, behind
 
 
@@ -194,7 +194,8 @@
     ]
     ahead = [
         remote(send.at[1, :, pl.ds(2, 6)], recv.at[1, :, pl.ds(2, 6)], sems, 1, where[1]),
-        remote(send.at[3, :, pl.ds(1, 7)], recv.at[3, :, pl.ds(1, 7)], sems, 3, where[3]),
+        remote(send.at[3, :, pl.ds(1, 1)], recv.at[3, :, pl.ds(1, 1)], sems, 3, where[3]),
+        remote(send.at[3, :, pl.ds(3, 5)], recv.at[3, :, pl.ds(3, 5)], sems, 6, where[3]),
     ]
     return ahead, behind
 
@@ -516,13 +517,16 @@
         gather_own(m, links[level, 0], links[level, 1], la, lb, ld)
         staples_own(la, lb, ld, lt, pc.at[level])
 
-    def forward(level):
+    def forward_ahead(level):
         la, lb, lc, ld, lt, lz = of(level, ga, gb, gc, gd, keep_t, keep_z)
-        ahead, behind = moves_u[level]
-        landed(ahead)
+        landed(moves_u[level][0])
         gather_ahead(m, recv_u.at[level], la, lb, lc, ld)
         staples_ahead(la, lb, lc, ld, lt, lz, sa.at[level], pb, pc.at[level], sd.at[level])
         csum[level, 0], csum[level, 1] = scatter_own(m, sa.at[level], pb, pc.at[level], sd.at[level])
+
+    def forward_behind(level):
+        la, lb, ld, lt = of(level, ga, gb, gd, keep_t)
+        behind = moves_u[level][1]
         landed(behind)
         gather_behind(m, recv_u.at[level], corner_u.at[level], la, lb, ld)
         staples_behind(la, lb, ld, lt, rim)
@@ -570,9 +574,10 @@
     before(1)
     sent(moves_u[0])
     start(moves_u[1])
-    forward(0)
+    forward_ahead(0)
+    forward_behind(0)
     moves_w0 = send_force(0)
-    finish(0, moves_w0, lambda: forward(1))
+    finish(0, moves_w0, lambda: (forward_ahead(1), forward_behind(1)))
     force_products(links.at[1], force, keep_d)
     moves_w1 = send_force(1)
     finish(1, moves_w1, lambda: None)
@@ -633,8 +638,8 @@
                 pltpu.SemaphoreType.DMA((3, 4)),
                 pltpu.SemaphoreType.DMA((2, 23)),
                 pltpu.SemaphoreType.DMA((2, 23)),
-                pltpu.SemaphoreType.DMA((2, 6)),
-                pltpu.SemaphoreType.DMA((2, 6)),
+                pltpu.SemaphoreType.DMA((2, 7)),
+                pltpu.SemaphoreType.DMA((2, 7)),
             ],
             compiler_params=pltpu.CompilerParams(
                 collective_id=0, has_side_effects=True, vmem_limit_bytes=48 * 1024 * 1024

time: 30.4 us -> 30.1 us (level)
  Pallas kernels: 29.6 us -> 29.2 us
    pallas_call x1, Pallas kernels: 29.6 us -> 29.2 us  [per_device(): pl.pallas_call(lambda *refs: kernel(counts, *refs), out_shape=jax.ShapeDt...]
where the time goes in v3:
time: 30.1 us; the launch traced here: 29.9 us
  Pallas kernels  29.2 us (97%)
  local copies, waits for them, and re-layouts  0.66 us (2%)
    pallas_call x1, Pallas kernels, per_device(): pl.pallas_call(lambda *refs: kernel(counts, *refs), out_shape=jax.ShapeDt...  29.2 us
    unnamed x1, local copies, waits for them, and re-layouts  0.66 us

profile of v3, /device:TPU:1, one launch (start us, length us, event | category | flops | bytes accessed | tf_op | source)
XLA Modules:
  0.0 29.9 jit_solution(4995630943725798731)
XLA Ops:
  0.0 29.2 %stout_back.1 = f32[4,18,4,128]{3,2,1,0:T(4,128)S(1)} custom-call(f32[4,18,4,128]{3,2,1,0:T(4,128)} %bitcast.5, f32[4,18,4,128]{3,2,1,0:T(4,128)} %bitcast.6, f32[4,18,4,128]{3,2,1,0:T(4,128)} %bitcast.7), custom_call_target="tpu_custom_call" | custom-call | tf_op jit(solution)/shard_map/stout_back/pallas_call | solution.py:598
  29.2 0.7 %copy.5 = f32[4,2,3,3,2,2,128]{6,5,4,3,2,1,0:T(2,128)} copy(f32[4,2,3,3,2,2,128]{6,5,4,3,2,1,0:T(2,128)S(1)} %bitcast.4) | data formatting | bytes 294912

commit v4 on v3

--- a/solution.py
+++ b/solution.py
@@ -143,6 +143,49 @@
     re = jnp.stack([jnp.stack([zero, r01, r02]), jnp.stack([-r01, zero, r12]), jnp.stack([-r02, -r12, zero])])
     im = jnp.stack([jnp.stack([d0, i01, i02]), jnp.stack([i01, d1, i12]), jnp.stack([i02, i12, d2])])
     return re, im
+
+
+def combine(terms):
+    total = None
+    for sign, coefficient, vector in terms:
+        term = coefficient * vector
+        if total is None:
+            total = term if sign > 0 else -term
+        else:
+            total = total + term if sign > 0 else total - term
+    return total
+
+
+def skew_sums(v, xr, xi, side):
+    pairs = {(0, 1): (v[3], v[4]), (0, 2): (v[5], v[6]), (1, 2): (v[7], v[8])}
+    out_r, out_i = [], []
+    for i in range(3):
+        re, im = [], []
+        for k in range(3):
+            if k == i:
+                continue
+            r, c = pairs[min(i, k), max(i, k)]
+            sign = side if i < k else -side
+            re += [(sign, r, xr[k]), (-1, c, xi[k])]
+            im += [(sign, r, xi[k]), (1, c, xr[k])]
+        re = sorted(re, key=lambda t: -t[0]) + [(-1, v[i], xi[i])]
+        im = [(1, v[i], xr[i])] + sorted(im, key=lambda t: -t[0])
+        out_r.append(combine(re))
+        out_i.append(combine(im))
+    axis = 0 if side > 0 else 1
+    return jnp.stack(out_r, axis=axis), jnp.stack(out_i, axis=axis)
+
+
+def skew_mul(v, x):
+    return skew_sums(v, lines(x[0]), lines(x[1]), 1)
+
+
+def mul_skew(x, v):
+    return skew_sums(v, columns(x[0]), columns(x[1]), -1)
+
+
+def dn_mul_skew(x, v):
+    return skew_sums(v, lines(x[0]), [-c for c in lines(x[1])], -1)
 
 
 def pack_sends(m, low, high, comps, send):
@@ -189,13 +232,13 @@
     behind = [
         remote(src.at[1, :, pl.ds(2, 1)], corner.at[:, pl.ds(1, 1)], sems, 4, where[4]),
         remote(src.at[1, :, pl.ds(5, 1)], corner.at[:, pl.ds(3, 1)], sems, 5, where[5]),
+        remote(send.at[2], recv.at[2], sems, 2, where[2]),
         remote(send.at[0], recv.at[0], sems, 0, where[0]),
-        remote(send.at[2], recv.at[2], sems, 2, where[2]),
     ]
     ahead = [
-        remote(send.at[1, :, pl.ds(2, 6)], recv.at[1, :, pl.ds(2, 6)], sems, 1, where[1]),
         remote(send.at[3, :, pl.ds(1, 1)], recv.at[3, :, pl.ds(1, 1)], sems, 3, where[3]),
         remote(send.at[3, :, pl.ds(3, 5)], recv.at[3, :, pl.ds(3, 5)], sems, 6, where[3]),
+        remote(send.at[1, :, pl.ds(2, 6)], recv.at[1, :, pl.ds(2, 6)], sems, 1, where[1]),
     ]
     return ahead, behind
 
@@ -305,27 +348,27 @@
 def forces_own(ga, gb, gd, keep_t, keep_z, sa, sd, wa, wb, wd, keep_n, zb, pa, pc, pd):
     def block(k):
         va, vd = wa[k], wd[k]
-        keep_n[k] = join(mul_dn(split(ga[k]), mul(skew_matrix(va - vd), split(gd[k]))))
-        pa[k] = join(mul(skew_matrix(vd), split(sa[k])))
-        pd[k] = join(mul(skew_matrix(va), split(sd[k])))
+        keep_n[k] = join(mul_dn(split(ga[k]), skew_mul(va - vd, split(gd[k]))))
+        pa[k] = join(skew_mul(vd, split(sa[k])))
+        pd[k] = join(skew_mul(va, split(sd[k])))
 
     each(0, 3, block)
     each(1, 3, lambda k: force_end(gb, keep_t, keep_z, wb, keep_n, zb, pc, k))
 
 
 def force_end(gb, keep_t, keep_z, wb, keep_n, zb, pc, k):
-    ob = skew_matrix(wb[k])
-    pc[k] = join(mul(sub(mul_dn(split(keep_t[k]), ob), dagger(split(keep_n[k]))), split(gb[k])))
-    zb[k] = join(mul(split(keep_z[k]), ob))
+    ob = wb[k]
+    pc[k] = join(mul(sub(dn_mul_skew(split(keep_t[k]), ob), dagger(split(keep_n[k]))), split(gb[k])))
+    zb[k] = join(mul_skew(split(keep_z[k]), ob))
 
 
 def forces_ahead(ga, gb, gc, gd, keep_t, keep_z, wb, wc, keep_n, zb, pa, pb, pc, pd):
     force_end(gb, keep_t, keep_z, wb, keep_n, zb, pc, 0)
 
     def block(k):
-        oc = skew_matrix(wc[k])
-        pb[k] = join(mul(sub(mul(split(keep_t[k]), oc), split(keep_n[k])), split(gc[k])))
-        q = sub(mul(oc, split(keep_z[k])), split(zb[k]))
+        oc = wc[k]
+        pb[k] = join(mul(sub(mul_skew(split(keep_t[k]), oc), split(keep_n[k])), split(gc[k])))
+        q = sub(skew_mul(oc, split(keep_z[k])), split(zb[k]))
         pa[k] = join(add(mul(split(gd[k]), q), split(pa[k])))
         pd[k] = join(add(mul_nd(split(ga[k]), q), split(pd[k])))
 
@@ -334,9 +377,9 @@
 
 def forces_behind(ga, gb, gd, keep_t, wa, wb, wd, rim):
     def block(k):
-        n = mul_dn(split(ga[k]), mul(skew_matrix(wa[k] - wd[k]), split(gd[k])))
+        n = mul_dn(split(ga[k]), skew_mul(wa[k] - wd[k], split(gd[k])))
         t = split(keep_t[k])
-        rim[k - 3] = join(mul(sub(mul_dn(t, skew_matrix(wb[k])), dagger(n)), split(gb[k])))
+        rim[k - 3] = join(mul(sub(dn_mul_skew(t, wb[k]), dagger(n)), split(gb[k])))
 
     each(3, 5, block)
 
@@ -359,7 +402,7 @@
         h = (parts[0] + parts[1] + parts[2]) * (1.0 / 3.0)
         parts = jnp.stack([v - h for v in parts[:3]] + parts[3:])
         b = skew_matrix(parts)
-        bb = mul(b, b)
+        bb = skew_mul(parts, b)
         p = 0.5 * (bb[0][0, 0] + bb[0][1, 1] + bb[0][2, 2])
         s = jnp.sum((b[1] * bb[0] - b[0] * bb[1]).reshape(9, 8, LANES), axis=0) * (1.0 / 3.0)
         w0, w1, w2, w3, w4 = weights(h)
@@ -444,7 +487,7 @@
         d2 = scaled(f2, d)
         back = dagger(d2)
         half = 0.5 * (d2[0] + back[0]), 0.5 * (d2[1] + back[1])
-        n = mul(b, half)
+        n = skew_mul(keep_b[k], half)
         d1 = scaled(f1, d)
         whole = (
             d1[0] - 2.0 * n[0] - gp * b[0] - gs * bb[1],
@@ -462,7 +505,7 @@
 def direct_forces(staple_sum, force, keep_e, omega, direct):
     def block(k):
         own = mul_dn(split(keep_e[k]), split(force[k]))
-        direct[k] = join(sub(own, mul(skew_matrix(omega[k]), split(staple_sum[k]))))
+        direct[k] = join(sub(own, skew_mul(omega[k], split(staple_sum[k]))))
 
     each(0, 2, block)
 

time: 30.1 us -> 30 us (level)
  no operation moved by 1% of the time
where the time goes in v4:
time: 30 us; the launch traced here: 29.8 us
  Pallas kernels  29.1 us (97%)
  local copies, waits for them, and re-layouts  0.66 us (2%)
    pallas_call x1, Pallas kernels, per_device(): pl.pallas_call(lambda *refs: kernel(counts, *refs), out_shape=jax.ShapeDt...  29.1 us
    unnamed x1, local copies, waits for them, and re-layouts  0.66 us

profile of v4, /device:TPU:1, one launch (start us, length us, event | category | flops | bytes accessed | tf_op | source)
XLA Modules:
  0.0 29.8 jit_solution(2368549182963112269)
XLA Ops:
  0.0 29.1 %stout_back.1 = f32[4,18,4,128]{3,2,1,0:T(4,128)S(1)} custom-call(f32[4,18,4,128]{3,2,1,0:T(4,128)} %bitcast.5, f32[4,18,4,128]{3,2,1,0:T(4,128)} %bitcast.6, f32[4,18,4,128]{3,2,1,0:T(4,128)} %bitcast.7), custom_call_target="tpu_custom_call" | custom-call | tf_op jit(solution)/shard_map/stout_back/pallas_call | solution.py:641
  29.1 0.7 %copy.5 = f32[4,2,3,3,2,2,128]{6,5,4,3,2,1,0:T(2,128)} copy(f32[4,2,3,3,2,2,128]{6,5,4,3,2,1,0:T(2,128)S(1)} %bitcast.4) | data formatting | bytes 294912

commit v5 on v4

--- a/solution.py
+++ b/solution.py
@@ -304,11 +304,8 @@
 
 
 def each(first, last, body):
-    def step(k, carry):
+    for k in range(first, last):
         body(k)
-        return carry
-
-    lax.fori_loop(first, last, step, 0)
 
 
 def staples_own(ga, gb, gd, keep_t, pc):
@@ -429,7 +426,8 @@
         keep_s[k] = jnp.stack([p, s, h, f1[0], f1[1], f2[0], f2[1]])
         return carry
 
-    lax.fori_loop(0, 2, block, 0)
+    for k in range(2):
+        block(k, 0)
 
 
 def force_products(links, force, keep_d):
@@ -499,7 +497,8 @@
         omega[k] = parts
         return carry
 
-    lax.fori_loop(0, 2, block, 0)
+    for k in range(2):
+        block(k, 0)
 
 
 def direct_forces(staple_sum, force, keep_e, omega, direct):

time: 30 us -> 29.7 us (0.990)
  no operation moved by 1% of the time
where the time goes in v5:
time: 29.7 us; the launch traced here: 29.6 us
  Pallas kernels  28.9 us (97%)
  local copies, waits for them, and re-layouts  0.66 us (2%)
    pallas_call x1, Pallas kernels, per_device(): pl.pallas_call(lambda *refs: kernel(counts, *refs), out_shape=jax.ShapeDt...  28.9 us
    unnamed x1, local copies, waits for them, and re-layouts  0.66 us

profile of v5, /device:TPU:1, one launch (start us, length us, event | category | flops | bytes accessed | tf_op | source)
XLA Modules:
  0.0 29.6 jit_solution(16240246414394838968)
XLA Ops:
  0.0 28.9 %stout_back.1 = f32[4,18,4,128]{3,2,1,0:T(4,128)S(1)} custom-call(f32[4,18,4,128]{3,2,1,0:T(4,128)} %bitcast.5, f32[4,18,4,128]{3,2,1,0:T(4,128)} %bitcast.6, f32[4,18,4,128]{3,2,1,0:T(4,128)} %bitcast.7), custom_call_target="tpu_custom_call" | custom-call | tf_op jit(solution)/shard_map/stout_back/pallas_call | solution.py:640
  28.9 0.7 %copy.5 = f32[4,2,3,3,2,2,128]{6,5,4,3,2,1,0:T(2,128)} copy(f32[4,2,3,3,2,2,128]{6,5,4,3,2,1,0:T(2,128)S(1)} %bitcast.4) | data formatting | bytes 294912
